TPU v7x, 512 devices: a whole 4x4x16 slice. The times are simulated.
512 devices in a mesh: row: 8 (over y, core), col: 8 (over z_lo), depth: 8 (over z_hi, x).
Axes of the slice: x: 4, y: 4, z: 16 (z_hi: 2, z_lo: 8; z = z_hi * 8 + z_lo), core: 2. Of those that a mesh axis runs over, the one named last changes fastest.
Arguments:
- tokens: bfloat16 [1024, 4096], P(('col', 'depth'), 'row'), may hold values from -6 to 6
- out_grad: bfloat16 [1024, 4096], P(('col', 'depth'), 'row'), may hold values from -2 to 2
- w_in: bfloat16 [4096, 14336], P('row', 'col'), may hold values from -0.09375 to 0.09375
- b_in: float32 [14336], P('col'), may hold values from -3 to 3
- w_out: bfloat16 [14336, 4096], P('col', 'row'), may hold values from -0.046875 to 0.046875
Outputs:
- block_out: bfloat16 [1024, 4096], P(('col', 'depth'), 'row')
- tokens_grad: bfloat16 [1024, 4096], P(('col', 'depth'), 'row')
- w_in_grad: bfloat16 [4096, 14336], P('row', ('col', 'depth'))
- w_out_grad: bfloat16 [14336, 4096], P(('col', 'depth'), 'row')
- b_in_grad: float32 [14336], P('col')
All inputs are finite; a program needn't handle non-finite values.
Results may differ from a plain program's by a relative error of at most 0.005.
Values may be sent and summed in bfloat16 or wider, within the bound.
No kernel may reach another device: no remote copies, remote signals or barrier semaphores. Data moves between devices by JAX's collectives and lax.ppermute only.
A program may use at most 64 MiB of HBM per device.

v0:
```python
import jax
import jax.numpy as jnp
from jax import lax
from jax.sharding import PartitionSpec as P

root_coeff = 0.7978845608028654
cubic_coeff = 0.044715


def gelu_parts(pre_act):
    inner_arg = root_coeff * (pre_act + cubic_coeff * pre_act * pre_act * pre_act)
    tangent = jnp.tanh(inner_arg)
    gelu_value = 0.5 * pre_act * (1.0 + tangent)
    gelu_slope = 0.5 * (1.0 + tangent) + 0.5 * pre_act * (1.0 - tangent * tangent) * root_coeff * (
        1.0 + 3.0 * cubic_coeff * pre_act * pre_act
    )
    return (gelu_value, gelu_slope)


def right_transposed(left_side, right_side):
    return lax.dot_general(
        left_side, right_side, (((1,), (1,)), ((), ())), preferred_element_type=jnp.float32
    )


def left_transposed(left_side, right_side):
    return lax.dot_general(
        left_side, right_side, (((0,), (0,)), ((), ())), preferred_element_type=jnp.float32
    )


def depth_rows(gathered, col_count, depth_index, depth_count):
    tile_rows = gathered.shape[0] // (col_count * depth_count)
    shaped = gathered.reshape(col_count, depth_count, tile_rows, gathered.shape[1])
    picked = lax.dynamic_index_in_dim(shaped, depth_index, 1, keepdims=False)
    return picked.reshape(col_count * tile_rows, gathered.shape[1])


def local(tokens, out_grad, w_in, b_in, w_out):
    col_count = lax.axis_size("col")
    depth_count = lax.axis_size("depth")
    tile_rows = tokens.shape[0]
    part_cols = w_in.shape[1] // depth_count
    depth_index = lax.axis_index("depth")
    all_input, all_grad = (
        lax.all_gather(tokens, ("col", "depth"), axis=0, tiled=True),
        lax.all_gather(out_grad, ("col", "depth"), axis=0, tiled=True),
    )
    plane_input = depth_rows(all_input, col_count, depth_index, depth_count)
    plane_grad = depth_rows(all_grad, col_count, depth_index, depth_count)
    pre_sum = lax.psum_scatter(
        jnp.dot(plane_input, w_in, preferred_element_type=jnp.float32),
        "row",
        scatter_dimension=0,
        tiled=True,
    )
    pre_share = pre_sum + b_in
    gelu_value, gelu_slope = gelu_parts(pre_share)
    plane_act = lax.all_gather(gelu_value.astype(jnp.bfloat16), "row", axis=0, tiled=True)
    block_out = lax.psum_scatter(
        jnp.dot(plane_act, w_out, preferred_element_type=jnp.float32),
        "col",
        scatter_dimension=0,
        tiled=True,
    ).astype(jnp.bfloat16)
    grad_share = lax.psum_scatter(
        right_transposed(plane_grad, w_out), "row", scatter_dimension=0, tiled=True
    )
    pre_grad = grad_share * gelu_slope
    plane_hgrad = lax.all_gather(pre_grad.astype(jnp.bfloat16), "row", axis=0, tiled=True)
    b_in_grad = lax.psum(jnp.sum(pre_grad, axis=0), ("row", "depth"))
    tokens_grad = lax.psum_scatter(
        right_transposed(plane_hgrad, w_in), "col", scatter_dimension=0, tiled=True
    ).astype(jnp.bfloat16)
    act_parts = lax.all_to_all(
        plane_act.reshape(col_count, tile_rows, w_in.shape[1]),
        "depth",
        split_axis=2,
        concat_axis=1,
        tiled=True,
    )
    act_parts = act_parts.reshape(-1, part_cols)
    hgrad_parts = lax.all_to_all(
        plane_hgrad.reshape(col_count, tile_rows, w_in.shape[1]),
        "depth",
        split_axis=2,
        concat_axis=1,
        tiled=True,
    )
    hgrad_parts = hgrad_parts.reshape(-1, part_cols)
    w_in_grad = left_transposed(all_input, hgrad_parts)
    w_out_grad = left_transposed(act_parts, all_grad)
    return (
        block_out,
        tokens_grad,
        w_in_grad.astype(jnp.bfloat16),
        w_out_grad.astype(jnp.bfloat16),
        b_in_grad,
    )


def solution(mesh):
    return jax.shard_map(
        local,
        mesh=mesh,
        in_specs=(
            P(("col", "depth"), "row"),
            P(("col", "depth"), "row"),
            P("row", "col"),
            P("col"),
            P("col", "row"),
        ),
        out_specs=(
            P(("col", "depth"), "row"),
            P(("col", "depth"), "row"),
            P("row", ("col", "depth")),
            P(("col", "depth"), "row"),
            P("col"),
        ),
        check_vma=False,
    )
```

profile of v0, /device:TPU:32, one launch (start us, length us, event | category | flops | bytes accessed | tf_op | source)
XLA Modules:
  0.0 1477.0 jit_solution(16970488687303766909)
XLA Ops:
  7.2 0.0 copy-start
  7.2 0.0 all-gather.3.cloned.1.call-start
  7.2 0.7 all-gather.3.cloned.1.call-update
  7.9 0.0 all-gather.5.cloned.1.call-start
  8.0 0.7 all-gather.5.cloned.1.call-update
  8.7 0.0 reduce-scatter.5.cloned.1.call-start
  8.7 482.7 %all-gather.3.cloned.1.call-done = bf16[1024,512]{1,0:T(8,128)(2,1)} async-done(((bf16[16,512]{1,0:T(8,128)(2,1)}), bf16[1024,512]{1,0:T(8,128)(2,1)}) %all-gather.3.cloned.1.call-update) | async-done | bytes 1048592 | tf_op jit(solution)/shard_map/all_gather | solution.py:46
  491.4 488.3 %all-gather.5.cloned.1.call-done = bf16[1024,512]{1,0:T(8,128)(2,1)} async-done(((bf16[16,512]{1,0:T(8,128)(2,1)}), bf16[1024,512]{1,0:T(8,128)(2,1)}) %all-gather.5.cloned.1.call-update) | async-done | bytes 1048592 | tf_op jit(solution)/shard_map/all_gather | solution.py:47
  979.8 1.0 constant_dynamic-slice_fusion
  980.8 0.0 copy-done
  980.8 1.4 fusion.9
  982.1 0.0 reduce-scatter.5.cloned.1.call-update
  982.2 0.0 reduce-scatter.9.cloned.1.call-start
  982.2 0.0 copy-start.2
  982.2 3.2 fusion.11
  985.4 0.0 reduce-scatter.9.cloned.1.call-update
  985.4 45.7 %reduce-scatter.5.cloned.1.call-done = f32[16,1792]{1,0:T(8,128)} async-done(((f32[128,1792]{1,0:T(8,128)}), f32[16,1792]{1,0:T(8,128)}) %reduce-scatter.5.cloned.1.call-update) | async-done | bytes 114704 | tf_op jit(solution)/shard_map/reduce_scatter | solution.py:51
  1031.2 41.2 %reduce-scatter.9.cloned.1.call-done = f32[16,1792]{1,0:T(8,128)} async-done(((f32[128,1792]{1,0:T(8,128)}), f32[16,1792]{1,0:T(8,128)}) %reduce-scatter.9.cloned.1.call-update) | async-done | bytes 114704 | tf_op jit(solution)/shard_map/reduce_scatter | solution.py:66
  1072.4 0.0 copy-done.2
  1072.4 1.1 fusion.7
  1073.5 13.0 all_gather.13
  1086.5 3.7 copy.15
  1090.2 6.0 reshape.49
  1096.2 13.8 all-to-all-start.1
  1109.9 13.0 all_gather.15
  1123.0 3.7 copy.12
  1126.6 5.9 reshape.47
  1132.6 9.8 all-to-all-done.1
  1142.4 4.7 all-to-all-start
  1147.0 0.0 reduce-scatter.11.cloned.1.call-start
  1147.1 1.4 fusion.12
  1148.5 0.0 reduce-scatter.11.cloned.1.call-update
  1148.5 0.0 reduce-scatter.7.cloned.1.call-start
  1148.6 2.6 fusion.10
  1151.2 0.0 reduce-scatter.7.cloned.1.call-update
  1151.2 295.6 %psum.7 = f32[1792]{0:T(1024)} all-reduce(f32[1792]{0:T(1024)S(1)} %get-tuple-element.5), channel_id=1, replica_groups=mesh['row'=8,'col'=8,'depth'=8] {'row','depth'}, use_global_device_ids=true, to_apply=%region_5.6 | all-reduce | flops 1792 | bytes 14336 | tf_op jit(solution)/shard_map/psum | solution.py:71
  1446.8 0.0 reduce-scatter.11.cloned.1.call-done
  1446.8 1.4 convert_element_type.24
  1448.2 1.4 convert_element_type.22
  1449.6 3.9 reshape.50
  1453.4 4.1 copy.17
  1457.5 0.0 all-to-all-done
  1457.5 5.1 reshape.48
  1462.6 4.1 copy.14
  1466.6 0.0 copy-start.1
  1466.6 2.4 convolution_convert_fusion
  1469.1 0.0 copy-done.1
  1469.1 1.1 fusion
  (1 shorter events, 0.0 us)
Async XLA Ops:
  7.2 973.6 %copy-start = (bf16[512,1792]{1,0:T(8,128)(2,1)S(1)}, bf16[512,1792]{1,0:T(8,128)(2,1)}, u32[]{:S(2)}) copy-start(bf16[512,1792]{1,0:T(8,128)(2,1)} %param.7) | copy-start | bytes 5505028
  7.2 484.3 %all-gather.3.cloned.1.call-start = ((), (), s32[]{:S(2)}) async-start(), calls=%async_computation.6 | async-start | bytes 1064960 | tf_op jit(solution)/shard_map/all_gather | solution.py:46
  7.9 971.9 %all-gather.5.cloned.1.call-start = ((), (), s32[]{:S(2)}) async-start(), calls=%async_computation.9 | async-start | bytes 1064960 | tf_op jit(solution)/shard_map/all_gather | solution.py:47
  8.7 1022.5 %reduce-scatter.5.cloned.1.call-start = ((), (), s32[]{:S(2)}) async-start(), calls=%async_computation.7 | async-start | bytes 1032192 | tf_op jit(solution)/shard_map/reduce_scatter | solution.py:51
  982.2 90.2 %reduce-scatter.9.cloned.1.call-start = ((), (), s32[]{:S(2)}) async-start(), calls=%async_computation.10 | async-start | bytes 1032192 | tf_op jit(solution)/shard_map/reduce_scatter | solution.py:66
  982.2 90.2 %copy-start.2 = (f32[1792]{0:T(1024)S(1)}, f32[1792]{0:T(1024)}, u32[]{:S(2)}) copy-start(f32[1792]{0:T(1024)} %param.8) | copy-start | bytes 21508
  1096.2 46.2 %all-to-all-start.1 = ((bf16[8,2,14336]{2,1,0:T(2,128)(2,1)}), bf16[8,2,14336]{2,1,0:T(2,128)(2,1)S(1)}, u32[]{:S(2)}, u32[]{:S(2)}) async-start(bf16[8,2,14336]{2,1,0:T(2,128)(2,1)} %reshape.49), calls=%async_computation.5 | async-start | bytes 917504 | tf_op jit(solution)/shard_map/all_to_all | solution.py:75
  1142.4 315.1 %all-to-all-start = ((bf16[8,2,14336]{2,1,0:T(2,128)(2,1)}), bf16[8,2,14336]{2,1,0:T(2,128)(2,1)}, u32[]{:S(2)}, u32[]{:S(2)}) async-start(bf16[8,2,14336]{2,1,0:T(2,128)(2,1)} %reshape.47), calls=%async_computation.4 | async-start | bytes 917504 | tf_op jit(solution)/shard_map/all_to_all | solution.py:83
  1147.0 299.8 %reduce-scatter.11.cloned.1.call-start = ((), (), s32[]{:S(2)}) async-start(), calls=%async_computation.11 | async-start | bytes 294912 | tf_op jit(solution)/shard_map/reduce_scatter | solution.py:72
  1148.5 299.7 %reduce-scatter.7.cloned.1.call-start = ((), (), s32[]{:S(2)}) async-start(), calls=%async_computation.8 | async-start | bytes 294912 | tf_op jit(solution)/shard_map/reduce_scatter | solution.py:60
  1466.6 2.4 copy-start.1
Sparse Core Ops, SparseCore 0:
  10.1 481.3 all-gather.2
  493.5 486.2 all-gather.4
  982.6 48.5 reduce-scatter.4
  1033.9 38.4 reduce-scatter.8
  1150.3 59.0 reduce-scatter.10
  1212.1 56.2 reduce-scatter.6
where the time goes:
time: 1480 us
  waiting for transfers between devices  1070 us (72%)
  blocking collectives  322 us (22%)
  local copies, waits for them, and re-layouts  37.3 us (3%)
  starting transfers between devices  18.7 us (1%)
    all_gather x1, waiting for transfers between devices, local(): lax.all_gather(out_grad, ('col', 'depth'), axis=0, tiled=True)  488 us
    all_gather x1, waiting for transfers between devices, local(): lax.all_gather(tokens, ('col', 'depth'), axis=0, tiled=True)  483 us
    psum x1, blocking collectives, local(): b_in_grad = lax.psum(jnp.sum(pre_grad, axis=0), ('row', 'depth'))  296 us
    reduce_scatter x1, waiting for transfers between devices, local(): lax.psum_scatter(jnp.dot(plane_input, w_in, preferred_element_type=jnp.fl...  45.7 us
    reduce_scatter x1, waiting for transfers between devices, local(): lax.psum_scatter(right_transposed(plane_grad, w_out), 'row', scatter_dime...  41.2 us
  transfers between devices with their start and end apart: 8, of which 5 were waited for; matrix products, arithmetic and copies ran while one was open for 2% of the time, Pallas kernels for 0%

commit v1 on v0

--- a/solution.py
+++ b/solution.py
@@ -43,7 +43,15 @@
     part_cols = w_in.shape[1] // depth_count
     depth_index = lax.axis_index("depth")
     all_input, all_grad = (
-        lax.all_gather(tokens, ("col", "depth"), axis=0, tiled=True),
+        jnp.concatenate(
+            jax.lax.all_to_all(
+                jnp.stack(jax.lax.psum(1, axis_name=("col", "depth")) * [tokens], axis=0),
+                concat_axis=0,
+                split_axis=0,
+                axis_name=("col", "depth"),
+            ),
+            0,
+        ),
         lax.all_gather(out_grad, ("col", "depth"), axis=0, tiled=True),
     )
     plane_input = depth_rows(all_input, col_count, depth_index, depth_count)

time: 1480 us -> 1010 us (0.68)
  waiting for transfers between devices: 1070 us -> 580 us
  starting transfers between devices: 18.7 us -> 36.7 us
    all_gather x1 -> x0, waiting for transfers between devices: 483 us -> none  [local(): lax.all_gather(tokens, ('col', 'depth'), axis=0, tiled=True)]
    all_to_all x0 -> x1, starting transfers between devices: none -> 18.2 us  [local(): jax.lax.all_to_all(jnp.stack(jax.lax.psum(1, axis_name=('col', 'depth'))...]
  transfers between devices with their start and end apart: 8 -> 8, of which waited for: 5 -> 4; matrix products, arithmetic and copies ran while one was open for 2% -> 3% of each run, Pallas kernels for 0% -> 0%
where the time goes in v1:
time: 1010 us
  waiting for transfers between devices  580 us (57%)
  blocking collectives  322 us (32%)
  local copies, waits for them, and re-layouts  40.1 us (4%)
  starting transfers between devices  36.7 us (4%)
  between operations  13.9 us (1%)
  matrix products  12 us (1%)
    all_gather x1, waiting for transfers between devices, local(): lax.all_gather(out_grad, ('col', 'depth'), axis=0, tiled=True)  483 us
    psum x1, blocking collectives, local(): b_in_grad = lax.psum(jnp.sum(pre_grad, axis=0), ('row', 'depth'))  296 us
    reduce_scatter x1, waiting for transfers between devices, local(): lax.psum_scatter(jnp.dot(plane_input, w_in, preferred_element_type=jnp.fl...  45.1 us
    reduce_scatter x1, waiting for transfers between devices, local(): lax.psum_scatter(right_transposed(plane_grad, w_out), 'row', scatter_dime...  41.4 us
    unnamed x14, local copies, waits for them, and re-layouts  20.9 us
  transfers between devices with their start and end apart: 8, of which 4 were waited for; matrix products, arithmetic and copies ran while one was open for 3% of the time, Pallas kernels for 0%

profile of v1, /device:TPU:32, one launch (start us, length us, event | category | flops | bytes accessed | tf_op | source)
XLA Modules:
  0.0 1007.7 jit_solution(3870342761068955431)
XLA Ops:
  7.2 0.0 copy-start
  7.2 2.0 stack.2
  9.1 18.2 %all-to-all-start = ((bf16[64,16,512]{2,1,0:T(8,128)(2,1)}), bf16[64,16,512]{2,1,0:T(8,128)(2,1)S(1)}, u32[]{:S(2)}, u32[]{:S(2)}) async-start(bf16[64,16,512]{2,1,0:T(8,128)(2,1)} %stack.2), calls=%async_computation | async-start | bytes 2097152 | tf_op jit(solution)/shard_map/all_to_all | solution.py:47
  27.4 0.0 all-gather.2.cloned.1.call-start
  27.4 0.7 all-gather.2.cloned.1.call-update
  28.1 0.0 reduce-scatter.5.cloned.1.call-start
  28.1 482.7 %all-gather.2.cloned.1.call-done = bf16[1024,512]{1,0:T(8,128)(2,1)} async-done(((bf16[16,512]{1,0:T(8,128)(2,1)}), bf16[1024,512]{1,0:T(8,128)(2,1)}) %all-gather.2.cloned.1.call-update) | async-done | bytes 1048592 | tf_op jit(solution)/shard_map/all_gather | solution.py:55
  510.8 0.0 all-to-all-done
  510.8 1.0 constant_dynamic-slice_fusion
  511.9 0.0 copy-done
  511.9 1.4 fusion.9
  513.2 0.0 reduce-scatter.5.cloned.1.call-update
  513.2 0.0 copy-done.1
  513.2 0.0 reduce-scatter.9.cloned.1.call-start
  513.3 0.0 copy-start.4
  513.3 3.2 fusion.11
  516.5 0.0 reduce-scatter.9.cloned.1.call-update
  516.5 45.1 %reduce-scatter.5.cloned.1.call-done = f32[16,1792]{1,0:T(8,128)} async-done(((f32[128,1792]{1,0:T(8,128)}), f32[16,1792]{1,0:T(8,128)}) %reduce-scatter.5.cloned.1.call-update) | async-done | bytes 114704 | tf_op jit(solution)/shard_map/reduce_scatter | solution.py:59
  561.6 41.4 %reduce-scatter.9.cloned.1.call-done = f32[16,1792]{1,0:T(8,128)} async-done(((f32[128,1792]{1,0:T(8,128)}), f32[16,1792]{1,0:T(8,128)}) %reduce-scatter.9.cloned.1.call-update) | async-done | bytes 114704 | tf_op jit(solution)/shard_map/reduce_scatter | solution.py:74
  603.0 0.0 copy-done.4
  603.0 1.1 fusion.7
  604.1 13.0 %all_gather.9 = bf16[128,1792]{1,0:T(8,128)(2,1)S(1)} all-gather(bf16[16,1792]{1,0:T(8,128)(2,1)S(1)} %get-tuple-element.7), channel_id=1, replica_groups=mesh['row'=8,'col'=8,'depth'=8] {'row'}, dimensions={0}, use_global_device_ids=true | all-gather | bytes 516096 | tf_op jit(solution)/shard_map/all_gather | solution.py:67
  617.1 3.7 copy.15
  620.8 5.9 reshape.51
  626.8 13.6 %all-to-all-start.2 = ((bf16[8,2,14336]{2,1,0:T(2,128)(2,1)}), bf16[8,2,14336]{2,1,0:T(2,128)(2,1)S(1)}, u32[]{:S(2)}, u32[]{:S(2)}) async-start(bf16[8,2,14336]{2,1,0:T(2,128)(2,1)} %reshape.51), calls=%async_computation.6 | async-start | bytes 917504 | tf_op jit(solution)/shard_map/all_to_all | solution.py:83
  640.4 13.0 %all_gather.11 = bf16[128,1792]{1,0:T(8,128)(2,1)S(1)} all-gather(bf16[16,1792]{1,0:T(8,128)(2,1)S(1)} %get-tuple-element.6), channel_id=1, replica_groups=mesh['row'=8,'col'=8,'depth'=8] {'row'}, dimensions={0}, use_global_device_ids=true | all-gather | bytes 516096 | tf_op jit(solution)/shard_map/all_gather | solution.py:78
  653.4 3.7 copy.12
  657.1 5.9 reshape.49
  663.1 9.8 all-to-all-done.2
  672.9 4.6 all-to-all-start.1
  677.5 0.0 reduce-scatter.11.cloned.1.call-start
  677.5 1.4 fusion.12
  679.0 0.0 reduce-scatter.11.cloned.1.call-update
  679.0 0.0 reduce-scatter.7.cloned.1.call-start
  679.0 2.6 fusion.10
  681.7 0.0 reduce-scatter.7.cloned.1.call-update
  681.7 295.6 %psum.7 = f32[1792]{0:T(1024)} all-reduce(f32[1792]{0:T(1024)S(1)} %get-tuple-element.5), channel_id=1, replica_groups=mesh['row'=8,'col'=8,'depth'=8] {'row','depth'}, use_global_device_ids=true, to_apply=%region_5.6 | all-reduce | flops 1792 | bytes 14336 | tf_op jit(solution)/shard_map/psum | solution.py:79
  977.3 1.4 convert_element_type.24
  978.6 1.4 convert_element_type.22
  980.0 3.9 reshape.52
  983.9 4.1 copy.17
  987.9 0.0 all-to-all-done.1
  987.9 5.1 reshape.50
  993.0 4.8 copy.14
  997.8 0.0 copy-done.2
  997.8 2.2 fusion
  1000.1 0.0 copy-done.3
  1000.1 1.1 convolution_convert_fusion
  (5 shorter events, 0.0 us)
Async XLA Ops:
  7.2 504.7 %copy-start = (bf16[512,1792]{1,0:T(8,128)(2,1)S(1)}, bf16[512,1792]{1,0:T(8,128)(2,1)}, u32[]{:S(2)}) copy-start(bf16[512,1792]{1,0:T(8,128)(2,1)} %param.7) | copy-start | bytes 5505028
  9.1 501.7 %all-to-all-start = ((bf16[64,16,512]{2,1,0:T(8,128)(2,1)}), bf16[64,16,512]{2,1,0:T(8,128)(2,1)S(1)}, u32[]{:S(2)}, u32[]{:S(2)}) async-start(bf16[64,16,512]{2,1,0:T(8,128)(2,1)} %stack.2), calls=%async_computation | async-start | bytes 2097152 | tf_op jit(solution)/shard_map/all_to_all | solution.py:47
  27.4 483.4 %all-gather.2.cloned.1.call-start = ((), (), s32[]{:S(2)}) async-start(), calls=%async_computation.9 | async-start | bytes 1064960 | tf_op jit(solution)/shard_map/all_gather | solution.py:55
  28.1 533.5 %reduce-scatter.5.cloned.1.call-start = ((), (), s32[]{:S(2)}) async-start(), calls=%async_computation.7 | async-start | bytes 1032192 | tf_op jit(solution)/shard_map/reduce_scatter | solution.py:59
  510.8 2.4 copy-start.1
  513.2 89.8 %reduce-scatter.9.cloned.1.call-start = ((), (), s32[]{:S(2)}) async-start(), calls=%async_computation.10 | async-start | bytes 1032192 | tf_op jit(solution)/shard_map/reduce_scatter | solution.py:74
  513.3 89.7 %copy-start.4 = (f32[1792]{0:T(1024)S(1)}, f32[1792]{0:T(1024)}, u32[]{:S(2)}) copy-start(f32[1792]{0:T(1024)} %param.8) | copy-start | bytes 21508
  626.8 46.1 %all-to-all-start.2 = ((bf16[8,2,14336]{2,1,0:T(2,128)(2,1)}), bf16[8,2,14336]{2,1,0:T(2,128)(2,1)S(1)}, u32[]{:S(2)}, u32[]{:S(2)}) async-start(bf16[8,2,14336]{2,1,0:T(2,128)(2,1)} %reshape.51), calls=%async_computation.6 | async-start | bytes 917504 | tf_op jit(solution)/shard_map/all_to_all | solution.py:83
  672.9 315.1 %all-to-all-start.1 = ((bf16[8,2,14336]{2,1,0:T(2,128)(2,1)}), bf16[8,2,14336]{2,1,0:T(2,128)(2,1)}, u32[]{:S(2)}, u32[]{:S(2)}) async-start(bf16[8,2,14336]{2,1,0:T(2,128)(2,1)} %reshape.49), calls=%async_computation.5 | async-start | bytes 917504 | tf_op jit(solution)/shard_map/all_to_all | solution.py:91
  677.5 299.8 %reduce-scatter.11.cloned.1.call-start = ((), (), s32[]{:S(2)}) async-start(), calls=%async_computation.11 | async-start | bytes 294912 | tf_op jit(solution)/shard_map/reduce_scatter | solution.py:80
  679.0 299.6 %reduce-scatter.7.cloned.1.call-start = ((), (), s32[]{:S(2)}) async-start(), calls=%async_computation.8 | async-start | bytes 294912 | tf_op jit(solution)/shard_map/reduce_scatter | solution.py:68
  993.0 4.8 copy-start.2
  997.8 2.2 copy-start.3
Sparse Core Ops, SparseCore 0:
  30.2 480.5 all-gather.1
  513.6 47.9 reduce-scatter.4
  564.4 38.5 reduce-scatter.8
  680.8 59.1 reduce-scatter.10
  742.6 56.2 reduce-scatter.6
